TPU v7x, 128 devices: a whole 4x4x4 slice. The times are simulated.
128 devices in a mesh: row: 16 (over z_lo, x, core), col: 8 (over z_hi, y).
Axes of the slice: x: 4, y: 4, z: 4 (z_hi: 2, z_lo: 2; z = z_hi * 2 + z_lo), core: 2. Of those that a mesh axis runs over, the one named last changes fastest.
Arguments:
- inverse_front: float32 [16384, 16384], P('row', 'col'), may hold values from -0.09375 to 0.09375
- factor: float32 [4096, 1024], P('row'), may hold values from -1.2 to 1.2
- unit_lower: float32 [2, 512, 512], replicated, may hold values from -0.25 to 0.25
- pivot_inverse: float32 [2, 512], replicated, may hold values from 0.5 to 4
- tile_list: int32 [2, 16], replicated, may hold values from 0 to 63, as said below
- tile_valid: int32 [2, 16], replicated, may hold values from 0 to 1, as said below
Outputs:
- inverse_column: float32 [16384, 1024], P('row')
- diagonal_block: float32 [2, 512, 512], replicated
Inputs may be any that keep to these rules, and one draw needn't show every extreme that they name: `tile_list`: each row names 16 different tile rows of the front in increasing order, exactly 1 of them among each aligned group of 4 tile rows, and the last tile row is always among them. `tile_valid`: each row holds at least one 1.
All inputs are finite; a program needn't handle non-finite values.
Results may differ from a plain program's by a relative error of at most 0.0001.
Values sent between devices are 32-bit elements; how exact they have to be, the bound alone decides.
A program may use at most 192 MiB of HBM per device.

v0:
```python
import jax
import jax.numpy as jnp
from jax import lax
from jax.sharding import PartitionSpec as P

B = 256
W = 512
NS = 2
NA = 16


def from_root(block, axis, owner):
    block = jnp.where(lax.axis_index(axis) == owner, block, jnp.zeros_like(block))
    return lax.psum(block, axis)


def inner_left(left, right):
    return lax.dot_general(
        left,
        right,
        (((0,), (0,)), ((), ())),
        precision=lax.Precision.HIGHEST,
        preferred_element_type=jnp.float32,
    )


def shards(inverse_front, factor, unit_lower, pivot_inverse, tile_list, tile_valid):
    row_count = lax.axis_size("row")
    col_count = lax.axis_size("col")
    row_span, col_span = inverse_front.shape
    row_index = lax.axis_index("row")
    col_index = lax.axis_index("col")
    identity = jnp.eye(W, dtype=jnp.float32)
    inverses = [jnp.tril(unit_lower[member], -1) + identity for member in range(NS)]

    def normalize(slab):
        return jnp.concatenate(
            [
                jnp.dot(
                    slab[:, member * W : (member + 1) * W],
                    inverses[member],
                    precision=lax.Precision.HIGHEST,
                    preferred_element_type=jnp.float32,
                )
                for member in range(NS)
            ],
            axis=1,
        )

    normalized = lax.all_gather(normalize(factor), "row", axis=0, tiled=True)
    slot_tiles = normalized.reshape(NA, B, NS, W)

    def place_tiles(first, number):
        global_tile = first + jnp.arange(number, dtype=jnp.int32)
        onehot = (
            (tile_list[:, None, :] == global_tile[None, :, None]) & (tile_valid[:, None, :] > 0)
        ).astype(jnp.float32)
        placed = jnp.einsum("sta,absw->tbsw", onehot, slot_tiles, precision=lax.Precision.HIGHEST)
        return (placed.reshape(number * B, NS * W), jnp.sum(onehot, axis=2))

    row_factor, row_chosen = place_tiles(row_index * (row_span // B), row_span // B)
    col_factor, col_chosen = place_tiles(col_index * (col_span // B), col_span // B)
    row_global = row_index * row_span + jnp.arange(row_span, dtype=jnp.int32)
    col_global = col_index * col_span + jnp.arange(col_span, dtype=jnp.int32)
    lower_part = jnp.where(row_global[:, None] >= col_global[None, :], inverse_front, 0.0)
    lower_prod = jnp.dot(
        lower_part, col_factor, precision=lax.Precision.HIGHEST, preferred_element_type=jnp.float32
    )
    strict = jnp.where(row_global[:, None] > col_global[None, :], inverse_front, 0.0)
    mirror_prod = inner_left(strict, row_factor)
    row_total = lax.psum(lower_prod, "col")
    col_total = lax.psum(mirror_prod, "row")
    grid_ratio = row_count // col_count
    offset = row_index % grid_ratio * row_span
    own_piece = lax.dynamic_slice_in_dim(col_total, offset, row_span, 0)
    mirrored = from_root(own_piece, "col", row_index // grid_ratio)
    keep_rows = jnp.repeat(row_chosen, B, axis=1)
    keep_mask = jnp.repeat(keep_rows.T, W, axis=1)
    column = -(row_total + mirrored) * keep_mask
    base_block = jnp.stack(
        [
            jnp.dot(
                inverses[member].T * pivot_inverse[member][None, :],
                inverses[member],
                precision=lax.Precision.HIGHEST,
                preferred_element_type=jnp.float32,
            )
            for member in range(NS)
        ]
    )
    diag_terms = jnp.stack(
        [
            inner_left(
                row_factor[:, member * W : (member + 1) * W],
                column[:, member * W : (member + 1) * W],
            )
            for member in range(NS)
        ]
    )
    diag_total = lax.psum(diag_terms, "row")
    diagonal_block = base_block - diag_total
    return (column, diagonal_block)


def solution(mesh):
    in_specs = (P("row", "col"), P("row", None), P(), P(), P(), P())
    out_specs = (P("row", None), P())
    return jax.shard_map(shards, mesh=mesh, in_specs=in_specs, out_specs=out_specs, check_vma=False)
```

profile of v0, /device:TPU:1, one launch (start us, length us, event | category | flops | bytes accessed | tf_op | source)
XLA Modules:
  0.0 620.7 jit_solution(13033368712311143179)
XLA Ops:
  7.2 0.0 copy-start.7
  7.2 0.0 all-gather.2.cloned.1.call-start
  7.2 3.3 convolution_bitcast_fusion.1
  10.5 3.3 convolution_bitcast_fusion.2
  13.8 1.0 pad_maximum_fusion.1
  14.8 0.0 all-gather.2.cloned.1.call-update
  14.9 0.0 all-reduce.4.cloned.1.call-start
  15.0 0.0 copy-done.7
  15.0 95.2 %all-gather.2.cloned.1.call-done = f32[4096,1024]{0,1:T(8,128)} async-done(((f32[256,1024]{0,1:T(8,128)}), f32[4096,1024]{0,1:T(8,128)}) %all-gather.2.cloned.1.call-update) | async-done | bytes 16777232 | tf_op jit(solution)/shard_map/all_gather | solution.py:50
  110.2 0.0 copy-start.5
  110.2 11.0 %copy.23 = f32[128,8,16,256]{3,2,1,0:T(8,128)S(1)} copy(f32[128,8,16,256]{3,1,2,0:T(8,128)} %bitcast.71) | data formatting | bytes 33554432
  121.2 0.0 copy-start
  121.2 0.0 copy-done.5
  121.2 6.5 %fusion.57 = f32[2,256,512,4]{1,3,2,0:T(4,128)S(1)} fusion(f32[16,256,2,512]{1,0,3,2:T(8,128)S(1)} %bitcast.67, s32[2,16]{1,0:T(2,128)S(1)} %copy-done.5, pred[2,16]{1,0:T(4,128)(4,1)S(1)} %broadcast_compare_fusion, s32[4]{0:T(128)S(1)} %iota_add_fusion.3), kind=kOutput, calls=%fused_computation.60 | convolution fusion | flops 201326848 | bytes 20971696 | tf_op jit(solution)/shard_map/sta,absw->tbsw/dot_general | solution.py:58
  127.7 0.0 copy-done
  127.7 1.0 copy.25
  128.8 0.0 copy-start.2
  128.8 2.0 copy-done.2
  130.8 57.2 %fusion = f32[2048,1024]{1,0:T(8,128)} fusion(f32[1024,1024]{0,1:T(8,128)S(1)} %bitcast.72, f32[1024,2048]{1,0:T(8,128)} %param.6, s32[2048]{0:T(1024)S(1)} %iota_add_fusion, s32[1024]{0:T(1024)S(1)} %iota_add_fusion.1), kind=kOutput, calls=%fused_computation | convolution fusion | flops 25773998080 | bytes 20983808 | tf_op jit(solution)/shard_map/dot_general | solution.py:18
  188.0 0.0 all-reduce.4.cloned.1.call-update
  188.0 0.0 all-reduce.8.cloned.1.call-start
  188.1 20.3 %copy.14 = f32[16,256,2,512]{3,0,1,2:T(8,128)} copy(f32[16,256,2,512]{1,0,3,2:T(8,128)} %bitcast.68) | data formatting | bytes 33554432 | tf_op jit(solution)/shard_map/reshape | solution.py:51
  208.4 11.9 %convolution_bitcast_fusion = f32[8,256,2,512]{3,0,1,2:T(8,128)} fusion(f32[16,256,2,512]{3,0,1,2:T(8,128)} %copy.14, s32[2,16]{1,0:T(2,128)S(1)} %copy-done.5, s32[8]{0:T(128)S(1)} %iota_add_fusion.4, pred[2,16]{1,0:T(4,128)(4,1)S(1)} %broadcast_compare_fusion), kind=kOutput, calls=%fused_computation.14 | convolution fusion | flops 402653696 | bytes 25166016 | tf_op jit(solution)/shard_map/sta,absw->tbsw/dot_general | solution.py:58
  220.4 10.5 %copy.15 = f32[8,256,2,512]{1,0,3,2:T(8,128)} copy(f32[8,256,2,512]{3,0,1,2:T(8,128)} %convolution_bitcast_fusion) | data formatting | bytes 16777216 | tf_op jit(solution)/shard_map/sta,absw->tbsw/transpose | solution.py:58
  230.8 10.9 %copy.24 = f32[128,8,8,256]{3,1,2,0:T(8,128)} copy(f32[128,8,8,256]{3,2,1,0:T(8,128)} %bitcast.69) | data formatting | bytes 16777216
  241.8 87.7 %all-reduce.4.cloned.1.call-done = f32[2048,1024]{1,0:T(8,128)} async-done(((f32[2048,1024]{1,0:T(8,128)}), f32[2048,1024]{1,0:T(8,128)}) %all-reduce.4.cloned.1.call-update) | async-done | bytes 8388624 | tf_op jit(solution)/shard_map/psum | solution.py:72
  329.5 33.9 %select_add_fusion = f32[1024,1024]{1,0:T(8,128)} fusion(f32[2048,1024]{1,0:T(8,128)} %all-reduce.4.cloned.1.call-done, s32[]{:T(128)S(6)} %select_n.43, pred[]{:T(512)S(6)} %eq.40, f32[2048,1024]{0,1:T(8,128)} %bitcast.77, f32[1024,2048]{1,0:T(8,128)} %param.6, s32[2048]{0:T(1024)S(1)} %iota_add_fusion, s32[1024]{0:T(1024)S(1)} %iota_add_fusion.1), kind=kOutput, calls=%fused_computation.7 | convolution fusion | flops 25776095232 | bytes 25178116 | tf_op jit(solution)/shard_map/dot_general | solution.py:66
  363.4 0.0 all-reduce.8.cloned.1.call-update
  363.4 0.2 all-reduce.6.cloned.1.call-start
  363.6 0.2 convert_reduce_fusion
  363.8 0.1 copy.17
  363.9 1.4 broadcast_in_dim.33
  365.3 3.0 copy.26
  368.3 106.8 %all-reduce.8.cloned.1.call-done = f32[1024,1024]{1,0:T(8,128)} async-done(((f32[1024,1024]{1,0:T(8,128)}), f32[1024,1024]{1,0:T(8,128)}) %all-reduce.8.cloned.1.call-update) | async-done | bytes 4194320 | tf_op jit(solution)/shard_map/psum | solution.py:71
  475.1 0.0 copy-start.3
  475.1 4.6 negate_multiply_fusion
  479.7 0.1 copy-done.3
  479.8 0.0 copy-start.1
  479.8 3.5 fusion.35
  483.3 3.5 fusion.30
  486.8 0.0 copy-done.1
  486.8 0.0 copy-start.6
  486.8 0.0 copy-start.4
  486.8 1.5 pad_maximum_fusion
  488.3 0.0 all-reduce.6.cloned.1.call-update
  488.3 0.0 copy-done.6
  488.4 0.8 copy-done.4
  489.2 2.3 fusion.27
  491.5 3.3 fusion.24
  494.8 115.6 %all-reduce.6.cloned.1.call-done = f32[2,512,512]{2,1,0:T(8,128)} async-done(((f32[2,512,512]{2,1,0:T(8,128)}), f32[2,512,512]{2,1,0:T(8,128)}) %all-reduce.6.cloned.1.call-update) | async-done | bytes 2097168 | tf_op jit(solution)/shard_map/psum | solution.py:100
  610.4 3.7 maximum_subtract_fusion
  (8 shorter events, 0.1 us)
Async XLA Ops:
  7.2 7.8 %copy-start.7 = (s32[2,16]{1,0:T(2,128)S(1)}, s32[2,16]{1,0:T(2,128)}, u32[]{:S(2)}) copy-start(s32[2,16]{1,0:T(2,128)} %param.11) | copy-start | bytes 388
  7.2 103.1 %all-gather.2.cloned.1.call-start = ((), (), s32[]{:S(2)}) async-start(), calls=%async_computation | async-start | bytes 17825792 | tf_op jit(solution)/shard_map/all_gather | solution.py:50
  14.9 314.6 %all-reduce.4.cloned.1.call-start = ((), (), s32[]{:S(2)}) async-start(), calls=%async_computation.1 | async-start | bytes 16777216 | tf_op jit(solution)/shard_map/psum | solution.py:72
  110.2 11.0 %copy-start.5 = (s32[2,16]{1,0:T(2,128)S(1)}, s32[2,16]{1,0:T(2,128)}, u32[]{:S(2)}) copy-start(s32[2,16]{1,0:T(2,128)} %param.10) | copy-start | bytes 388
  121.2 6.5 %copy-start = (f32[128,8,16,256]{3,2,1,0:T(8,128)}, f32[128,8,16,256]{3,2,1,0:T(8,128)S(1)}, u32[]{:S(2)}) copy-start(f32[128,8,16,256]{3,2,1,0:T(8,128)S(1)} %copy.23) | copy-start | bytes 50331652
  128.8 2.1 copy-start.2
  188.0 287.1 %all-reduce.8.cloned.1.call-start = ((), (), s32[]{:S(2)}) async-start(), calls=%async_computation.3 | async-start | bytes 8388608 | tf_op jit(solution)/shard_map/psum | solution.py:71
  363.4 247.0 %all-reduce.6.cloned.1.call-start = ((), (), s32[]{:S(2)}) async-start(), calls=%async_computation.2 | async-start | bytes 4194304 | tf_op jit(solution)/shard_map/psum | solution.py:100
  475.1 4.6 copy-start.3
  479.8 7.0 %copy-start.1 = (f32[1024,1024]{1,0:T(8,128)}, f32[1024,1024]{1,0:T(8,128)S(1)}, u32[]{:S(2)}) copy-start(f32[1024,1024]{1,0:T(8,128)S(1)} %negate_multiply_fusion) | copy-start | bytes 12582916
  486.8 1.5 copy-start.6
  486.8 2.4 copy-start.4
Sparse Core Ops, SparseCore 0:
  15.0 95.2 all-gather.1
  188.1 141.3 all-reduce.3
  363.5 111.5 all-reduce.7
  488.5 121.8 all-reduce.5
where the time goes:
time: 629 us; the launch traced here: 621 us
  waiting for transfers between devices  405 us (64%)
  matrix products  129 us (21%)
  local copies, waits for them, and re-layouts  61.2 us (10%)
  between operations  14.2 us (2%)
  other arithmetic  10.9 us (2%)
    psum x1, waiting for transfers between devices, shards(): diag_total = lax.psum(diag_terms, 'row')  116 us
    psum x1, waiting for transfers between devices, shards(): row_total = lax.psum(lower_prod, 'col')  107 us
    all_gather x1, waiting for transfers between devices, shards(): normalized = lax.all_gather(normalize(factor), 'row', axis=0, tiled=True)  95.2 us
    psum x1, waiting for transfers between devices, shards(): col_total = lax.psum(mirror_prod, 'row')  87.7 us
    dot_general x3, matrix products, inner_left(): lax.dot_general(left, right, (((0,), (0,)), ((), ())), precision=lax.Prec...  64.2 us
    dot_general x1, matrix products, shards(): jnp.dot(lower_part, col_factor, precision=lax.Precision.HIGHEST, preferre...  33.9 us
    unnamed x20, local copies, waits for them, and re-layouts  28.9 us
    reshape x1, local copies, waits for them, and re-layouts, shards(): slot_tiles = normalized.reshape(NA, B, NS, W)  20.3 us
  transfers between devices with their start and end apart: 4, of which 4 were waited for; matrix products, arithmetic and copies ran while one was open for 10% of the time, Pallas kernels for 0%

commit v1 on v0

--- a/solution.py
+++ b/solution.py
@@ -47,7 +47,9 @@
             axis=1,
         )
 
-    normalized = lax.all_gather(normalize(factor), "row", axis=0, tiled=True)
+    normalized = jnp.concatenate(
+        lax.all_to_all(jnp.stack([normalize(factor)] * lax.axis_size("row")), "row", 0, 0), axis=0
+    )
     slot_tiles = normalized.reshape(NA, B, NS, W)
 
     def place_tiles(first, number):

time: 629 us -> 758 us (1.21)
  waiting for transfers between devices: 405 us -> 556 us
  matrix products: 129 us -> 105 us
    all_to_all x0 -> x1, waiting for transfers between devices: none -> 224 us  [shards(): lax.all_to_all(jnp.stack([normalize(factor)] * lax.axis_size('row')), 'ro...]
    all_gather x1 -> x0, waiting for transfers between devices: 95.2 us -> none  [shards(): normalized = lax.all_gather(normalize(factor), 'row', axis=0, tiled=True)]
    another operation x0 -> x2, local copies, waits for them, and re-layouts: none -> 27.6 us  [the longest x1 20.3 us: shards(): slot_tiles = normalized.reshape(NA, B, NS, W)]
    dot_general x3, matrix products: 64.2 us -> 37.3 us  [inner_left(): lax.dot_general(left, right, (((0,), (0,)), ((), ())), precision=lax.Prec...]
    psum x1, waiting for transfers between devices: 87.7 us -> 110 us  [shards(): col_total = lax.psum(mirror_prod, 'row')]
    reshape x1 -> x0, local copies, waits for them, and re-layouts: 20.3 us -> none  [shards(): slot_tiles = normalized.reshape(NA, B, NS, W)]
    unnamed x20 -> x21, local copies, waits for them, and re-layouts: 28.9 us -> 17.6 us
  transfers between devices with their start and end apart: 4 -> 4, of which waited for: 4 -> 4; matrix products, arithmetic and copies ran while one was open for 10% -> 6% of each run, Pallas kernels for 0% -> 0%
where the time goes in v1:
time: 758 us; the launch traced here: 753 us
  waiting for transfers between devices  556 us (73%)
  matrix products  105 us (14%)
  local copies, waits for them, and re-layouts  60.7 us (8%)
  between operations  14.2 us (2%)
  other arithmetic  9.98 us (1%)
  starting transfers between devices  7.58 us (1%)
    all_to_all x1, waiting for transfers between devices, shards(): lax.all_to_all(jnp.stack([normalize(factor)] * lax.axis_size('row')), 'ro...  224 us
    psum x1, waiting for transfers between devices, shards(): diag_total = lax.psum(diag_terms, 'row')  115 us
    psum x1, waiting for transfers between devices, shards(): col_total = lax.psum(mirror_prod, 'row')  110 us
    psum x1, waiting for transfers between devices, shards(): row_total = lax.psum(lower_prod, 'col')  107 us
    dot_general x3, matrix products, inner_left(): lax.dot_general(left, right, (((0,), (0,)), ((), ())), precision=lax.Prec...  37.3 us
    dot_general x1, matrix products, shards(): jnp.dot(lower_part, col_factor, precision=lax.Precision.HIGHEST, preferre...  33.9 us
    dot_general x2, matrix products, place_tiles(): jnp.einsum('sta,absw->tbsw', onehot, slot_tiles, precision=lax.Precision....  21.5 us
    another operation x1, local copies, waits for them, and re-layouts, shards(): slot_tiles = normalized.reshape(NA, B, NS, W)  20.3 us
  transfers between devices with their start and end apart: 4, of which 4 were waited for; matrix products, arithmetic and copies ran while one was open for 6% of the time, Pallas kernels for 0%

profile of v1, /device:TPU:1, one launch (start us, length us, event | category | flops | bytes accessed | tf_op | source)
XLA Modules:
  0.0 753.2 jit_solution(11226185220218540625)
XLA Ops:
  7.2 3.3 convolution_bitcast_fusion.2
  10.5 3.3 convolution_bitcast_fusion.3
  13.7 0.1 pad_maximum_fusion.1
  13.8 7.4 stack.14
  21.2 0.0 copy-start.6
  21.2 7.3 all-to-all-start
  28.5 0.2 all-reduce.4.cloned.1.call-start
  28.7 0.0 copy-done.6
  28.8 224.0 %all-to-all-done = f32[16,256,1024]{1,2,0:T(8,128)} async-done(((f32[16,256,1024]{1,2,0:T(8,128)}), f32[16,256,1024]{1,2,0:T(8,128)}, u32[]{:S(2)}, u32[]{:S(2)}) %all-to-all-start) | async-done | bytes 16777248 | tf_op jit(solution)/shard_map/all_to_all | solution.py:51
  252.8 0.0 copy-start.4
  252.8 20.3 %copy.13 = f32[16,256,2,512]{3,0,1,2:T(8,128)} copy(f32[16,256,2,512]{1,3,2,0:T(8,128)} %bitcast.4) | data formatting | bytes 33554432 | tf_op jit(solution)/shard_map/reshape;reshape | solution.py:53
  273.1 0.0 copy-done.4
  273.1 9.7 %convolution_bitcast_fusion.1 = f32[4,256,2,512]{3,0,1,2:T(4,128)S(1)} fusion(f32[16,256,2,512]{3,0,1,2:T(8,128)} %copy.13, s32[2,16]{1,0:T(2,128)S(1)} %copy-done.4, pred[2,16]{1,0:T(4,128)(4,1)S(1)} %broadcast_compare_fusion, s32[4]{0:T(128)S(1)} %iota_add_fusion.3), kind=kOutput, calls=%fused_computation.15 | convolution fusion | flops 201326848 | bytes 20971696 | tf_op jit(solution)/shard_map/sta,absw->tbsw/dot_general | solution.py:60
  282.8 0.0 slice-start
  282.8 3.2 copy.16
  286.0 0.0 slice-start.1
  286.0 1.0 copy.21
  287.1 0.0 copy-start.1
  287.1 1.9 copy-done.1
  289.0 0.0 slice-done
  289.0 0.0 slice-done.1
  289.0 30.1 %fusion = f32[2048,1024]{1,0:T(8,128)} fusion(f32[1024,1024]{1,0:T(8,128)S(1)} %bitcast.64, f32[1024,2048]{1,0:T(8,128)S(1)} %bitcast.74, s32[2048]{0:T(1024)S(1)} %iota_add_fusion, s32[1024]{0:T(1024)S(1)} %iota_add_fusion.1), kind=kOutput, calls=%fused_computation | convolution fusion | flops 25773998080 | bytes 20983808 | tf_op jit(solution)/shard_map/dot_general | solution.py:18
  319.1 0.0 all-reduce.4.cloned.1.call-update
  319.2 0.0 all-reduce.8.cloned.1.call-start
  319.2 11.8 %convolution_bitcast_fusion = f32[8,256,2,512]{3,0,1,2:T(8,128)} fusion(f32[16,256,2,512]{3,0,1,2:T(8,128)} %copy.13, s32[2,16]{1,0:T(2,128)S(1)} %copy-done.4, s32[8]{0:T(128)S(1)} %iota_add_fusion.4, pred[2,16]{1,0:T(4,128)(4,1)S(1)} %broadcast_compare_fusion), kind=kOutput, calls=%fused_computation.14 | convolution fusion | flops 402653696 | bytes 25166016 | tf_op jit(solution)/shard_map/sta,absw->tbsw/dot_general | solution.py:60
  331.1 10.5 %copy.14 = f32[8,256,2,512]{1,0,3,2:T(8,128)} copy(f32[8,256,2,512]{3,0,1,2:T(8,128)} %convolution_bitcast_fusion) | data formatting | bytes 16777216 | tf_op jit(solution)/shard_map/sta,absw->tbsw/transpose | solution.py:60
  341.5 10.7 %copy.20 = f32[128,8,8,256]{3,1,2,0:T(8,128)} copy(f32[128,8,8,256]{3,2,1,0:T(8,128)} %bitcast.62) | data formatting | bytes 16777216
  352.3 109.6 %all-reduce.4.cloned.1.call-done = f32[2048,1024]{1,0:T(8,128)} async-done(((f32[2048,1024]{1,0:T(8,128)}), f32[2048,1024]{1,0:T(8,128)}) %all-reduce.4.cloned.1.call-update) | async-done | bytes 8388624 | tf_op jit(solution)/shard_map/psum | solution.py:74
  461.8 33.9 %select_add_fusion = f32[1024,1024]{1,0:T(8,128)} fusion(f32[2048,1024]{1,0:T(8,128)} %all-reduce.4.cloned.1.call-done, s32[]{:T(128)S(6)} %select_n.43, pred[]{:T(512)S(6)} %eq.40, f32[2048,1024]{0,1:T(8,128)} %bitcast.69, f32[1024,2048]{1,0:T(8,128)} %param.6, s32[2048]{0:T(1024)S(1)} %iota_add_fusion, s32[1024]{0:T(1024)S(1)} %iota_add_fusion.1), kind=kOutput, calls=%fused_computation.7 | convolution fusion | flops 25776095232 | bytes 25178116 | tf_op jit(solution)/shard_map/dot_general | solution.py:68
  495.7 0.0 all-reduce.8.cloned.1.call-update
  495.7 0.0 all-reduce.6.cloned.1.call-start
  495.8 0.2 convert_reduce_fusion
  495.9 0.1 copy.17
  496.1 1.6 broadcast_in_dim.33
  497.6 3.0 copy.22
  500.6 106.7 %all-reduce.8.cloned.1.call-done = f32[1024,1024]{1,0:T(8,128)} async-done(((f32[1024,1024]{1,0:T(8,128)}), f32[1024,1024]{1,0:T(8,128)}) %all-reduce.8.cloned.1.call-update) | async-done | bytes 4194320 | tf_op jit(solution)/shard_map/psum | solution.py:73
  607.4 0.0 copy-start.2
  607.4 4.6 negate_multiply_fusion
  612.0 0.1 copy-done.2
  612.0 0.0 copy-start
  612.0 3.6 fusion.30
  615.6 3.6 fusion.35
  619.2 0.0 copy-done
  619.2 0.0 copy-start.5
  619.2 0.0 copy-start.3
  619.3 1.5 pad_maximum_fusion
  620.7 0.0 all-reduce.6.cloned.1.call-update
  620.8 0.0 copy-done.5
  620.8 0.8 copy-done.3
  621.6 2.3 fusion.24
  623.9 3.5 fusion.27
  627.4 115.3 %all-reduce.6.cloned.1.call-done = f32[2,512,512]{2,1,0:T(8,128)} async-done(((f32[2,512,512]{2,1,0:T(8,128)}), f32[2,512,512]{2,1,0:T(8,128)}) %all-reduce.6.cloned.1.call-update) | async-done | bytes 2097168 | tf_op jit(solution)/shard_map/psum | solution.py:102
  742.8 3.7 maximum_subtract_fusion
  (9 shorter events, 0.1 us)
Async XLA Ops:
  21.2 7.6 %copy-start.6 = (s32[2,16]{1,0:T(2,128)S(1)}, s32[2,16]{1,0:T(2,128)}, u32[]{:S(2)}) copy-start(s32[2,16]{1,0:T(2,128)} %param.11) | copy-start | bytes 388
  21.2 231.6 %all-to-all-start = ((f32[16,256,1024]{1,2,0:T(8,128)}), f32[16,256,1024]{1,2,0:T(8,128)}, u32[]{:S(2)}, u32[]{:S(2)}) async-start(f32[16,256,1024]{1,2,0:T(8,128)} %stack.14), calls=%async_computation | async-start | bytes 33554432 | tf_op jit(solution)/shard_map/all_to_all | solution.py:51
  28.5 433.3 %all-reduce.4.cloned.1.call-start = ((), (), s32[]{:S(2)}) async-start(), calls=%async_computation.1 | async-start | bytes 16777216 | tf_op jit(solution)/shard_map/psum | solution.py:74
  252.8 20.3 %copy-start.4 = (s32[2,16]{1,0:T(2,128)S(1)}, s32[2,16]{1,0:T(2,128)}, u32[]{:S(2)}) copy-start(s32[2,16]{1,0:T(2,128)} %param.10) | copy-start | bytes 388
  282.8 6.3 slice-start
  286.0 3.0 slice-start.1
  287.1 2.0 copy-start.1
  319.2 288.2 %all-reduce.8.cloned.1.call-start = ((), (), s32[]{:S(2)}) async-start(), calls=%async_computation.3 | async-start | bytes 8388608 | tf_op jit(solution)/shard_map/psum | solution.py:73
  495.7 247.1 %all-reduce.6.cloned.1.call-start = ((), (), s32[]{:S(2)}) async-start(), calls=%async_computation.2 | async-start | bytes 4194304 | tf_op jit(solution)/shard_map/psum | solution.py:102
  607.4 4.6 copy-start.2
  612.0 7.2 copy-start
  619.2 1.5 copy-start.5
  619.2 2.4 copy-start.3
Sparse Core Ops, SparseCore 0:
  319.3 142.4 all-reduce.3
  495.8 111.5 all-reduce.7
  620.9 121.8 all-reduce.5
